TPU v7x, 32 devices: a whole 2x2x4 slice. The times are simulated.
32 devices in a mesh: lat: 4 (over y, x), lon: 8 (over z, core).
Axes of the slice: x: 2, y: 2, z: 4, core: 2. Of those that a mesh axis runs over, the one named last changes fastest.
Arguments:
- grad_rows: bfloat16 [32768, 128], P(('lat', 'lon')), may hold values from -6 to 6
- owner: int32 [32768, 1], P(('lat', 'lon')), may hold values from 0 to 31; in each aligned block of 1024 rows (0 to 1023, 1024 to 2047, ...) at most 64 rows name the same one
- lat_offset: int32 [32768], P(('lat', 'lon')), may hold values from 0 to 63
- lon_offset: int32 [32768], P(('lat', 'lon')), may hold values from 0 to 127
- position: bfloat16 [32768, 2], P(('lat', 'lon')), may hold values from 0 to 1
- live_count: int32 [32], P(('lat', 'lon')), may hold values from 512 to 1024
- features: bfloat16 [256, 1024, 128], P('lat', 'lon'), may hold values from -6 to 6
- conv_weight: bfloat16 [3, 3, 128, 128], replicated, may hold values from -0.1875 to 0.1875
Outputs:
- input_grad: bfloat16 [256, 1024, 128], P('lat', 'lon')
- weight_grad: float32 [3, 3, 128, 128], replicated
Inputs may be any that keep to these rules, and one draw needn't show every extreme that they name: `owner`: among the 1024 rows of one device no tile is named more than 64 times, a bound that some block reaches. `live_count`: entry k counts the real rows among the rows of device k, which come first.
All inputs are finite; a program needn't handle non-finite values.
Results may differ from a plain program's by a relative error of at most 0.012.
Values may be sent and summed in bfloat16 or wider, within the bound.
A program may use at most 128 MiB of HBM per device.

v0:
```python
import math
import jax
import jax.numpy as jnp
from jax import lax
from jax.sharding import PartitionSpec as P

rbf_scale = 1.5


def padded_2(cells, sides, width, closed):
    for axis, dim in sides:
        count = lax.axis_size(axis)
        ends = count if closed else count - 1
        head = lax.slice_in_dim(cells, 0, width, axis=dim)
        tail = lax.slice_in_dim(cells, cells.shape[dim] - width, cells.shape[dim], axis=dim)
        cells = jnp.concatenate(
            [
                lax.ppermute(tail, axis, [(i, (i + 1) % count) for i in range(ends)]),
                cells,
                lax.ppermute(head, axis, [((i + 1) % count, i) for i in range(ends)]),
            ],
            axis=dim,
        )
    return cells


def profile(frac):
    tap_index = jnp.arange(8).astype(frac.dtype)
    return jnp.exp(
        -jnp.square(tap_index[None, :] - 3.0 - frac[:, None]) / (2.0 * rbf_scale * rbf_scale)
    )


def clear_rim(padded):
    lat_index = lax.axis_index("lat")
    lat_count = lax.axis_size("lat")
    row_line = jnp.arange(padded.shape[0], dtype=jnp.int32)
    masked = (row_line == 0) & (lat_index == 0) | (row_line == padded.shape[0] - 1) & (
        lat_index == lat_count - 1
    )
    return jnp.where(masked[:, None, None], jnp.zeros_like(padded), padded)


def tap_matrix(offsets, weights, extent):
    tap_ints = jnp.arange(8, dtype=jnp.int32)
    cells = offsets[:, None] + tap_ints[None, :] + 1
    line = jnp.arange(extent, dtype=jnp.int32)
    picked = jnp.where(
        cells[:, :, None] == line[None, None, :], weights.astype(jnp.float32)[:, :, None], 0.0
    )
    return jnp.sum(picked, axis=1).astype(jnp.bfloat16)


def shards(grad_rows, owner, lat_offset, lon_offset, position, live_count, features, conv_weight):
    lat_total = lax.axis_size("lat")
    lon_total = lax.axis_size("lon")
    device_total = lat_total * lon_total
    row_total = grad_rows.shape[0]
    channels = grad_rows.shape[1]
    tile_lat = features.shape[0]
    tile_lon = features.shape[1]
    capacity = max(2, 2 * row_total // device_total)
    input_padded = clear_rim(padded_2(features, (("lat", 0), ("lon", 1)), 1, True))
    owner_tile = owner[:, 0]
    is_live = jnp.arange(row_total, dtype=jnp.int32) < live_count[0]
    matches = (
        (owner_tile[:, None] == jnp.arange(device_total, dtype=jnp.int32)[None, :])
        & is_live[:, None]
    ).astype(jnp.int32)
    earlier = jnp.cumsum(matches, axis=0) - matches
    slot_rank = jnp.sum(earlier * matches, axis=1)
    slot_index = jnp.where(is_live, owner_tile * capacity + slot_rank, device_total * capacity)
    outgoing = (
        jnp.zeros((device_total * capacity, channels), jnp.bfloat16)
        .at[slot_index]
        .set(grad_rows, mode="drop")
    )
    geometry = jnp.stack(
        [
            position[:, 0],
            position[:, 1],
            lat_offset.astype(jnp.bfloat16),
            lon_offset.astype(jnp.bfloat16),
        ],
        axis=1,
    )
    place_out = (
        jnp.zeros((device_total * capacity, 4), jnp.bfloat16)
        .at[slot_index]
        .set(geometry, mode="drop")
    )
    incoming, place_in = (
        lax.all_to_all(
            outgoing.reshape(device_total, capacity, channels),
            ("lat", "lon"),
            split_axis=0,
            concat_axis=0,
            tiled=True,
        ),
        lax.all_to_all(
            place_out.reshape(device_total, capacity, 4),
            ("lat", "lon"),
            split_axis=0,
            concat_axis=0,
            tiled=True,
        ),
    )
    incoming = incoming.reshape(-1, channels)
    place_in = place_in.reshape(-1, 4).astype(jnp.float32)
    padded_lat = tile_lat + 8
    padded_lon = tile_lon + 8
    slot_total = incoming.shape[0]
    block_rows = math.gcd(slot_total, 256)

    def accumulate(canvas, payload):
        rows_blk, place_blk = payload
        lat_weight = profile(place_blk[:, 0]).astype(jnp.bfloat16)
        lon_weight = profile(place_blk[:, 1]).astype(jnp.bfloat16)
        lat_matrix = tap_matrix(place_blk[:, 2].astype(jnp.int32), lat_weight, padded_lat)
        lon_matrix = tap_matrix(place_blk[:, 3].astype(jnp.int32), lon_weight, padded_lon)
        spread = (lon_matrix[:, :, None] * rows_blk[:, None, :]).reshape(
            rows_blk.shape[0], padded_lon * channels
        )
        canvas = canvas + lax.dot_general(
            lat_matrix, spread, (((0,), (0,)), ((), ())), preferred_element_type=jnp.float32
        )
        return (canvas, None)

    canvas, _ = lax.scan(
        accumulate,
        jnp.zeros((padded_lat, padded_lon * channels), jnp.float32),
        (incoming.reshape(-1, block_rows, channels), place_in.reshape(-1, block_rows, 4)),
    )
    canvas = canvas.reshape(padded_lat, padded_lon, channels)
    edge_rows = jnp.concatenate([canvas[:5], canvas[-5:]], axis=0)
    edge_rows = padded_2(edge_rows.astype(jnp.bfloat16), (("lat", 0),), 5, False).astype(
        edge_rows.dtype
    )
    inner = canvas[4:-4]
    inner = inner.at[:4].add(edge_rows[1:5]).at[-4:].add(edge_rows[15:19])
    rim_top = edge_rows[0] + canvas[3]
    rim_bottom = canvas[-4] + edge_rows[19]
    tall = jnp.concatenate([rim_top[None], inner, rim_bottom[None]], axis=0)
    side_cols = jnp.concatenate([tall[:, :5], tall[:, -5:]], axis=1)
    side_cols = padded_2(side_cols.astype(jnp.bfloat16), (("lon", 1),), 5, True).astype(
        side_cols.dtype
    )
    middle = tall[:, 4:-4]
    middle = middle.at[:, :4].add(side_cols[:, 1:5]).at[:, -4:].add(side_cols[:, 15:19])
    rim_left = side_cols[:, 0] + tall[:, 3]
    rim_right = tall[:, -4] + side_cols[:, 19]
    whole = jnp.concatenate([rim_left[:, None], middle, rim_right[:, None]], axis=1)
    grid_padded = clear_rim(whole.astype(jnp.bfloat16))
    grid_grad = grid_padded[1:-1, 1:-1]
    flat_grad = grid_grad.reshape(-1, channels)
    input_grad = jnp.zeros((tile_lat * tile_lon, channels), jnp.float32)
    weight_parts = []
    for a in range(3):
        for b in range(3):
            shifted = grid_padded[2 - a : 2 - a + tile_lat, 2 - b : 2 - b + tile_lon].reshape(
                -1, channels
            )
            input_grad = input_grad + lax.dot_general(
                shifted,
                conv_weight[a, b],
                (((1,), (1,)), ((), ())),
                preferred_element_type=jnp.float32,
            )
            window = input_padded[a : a + tile_lat, b : b + tile_lon].reshape(-1, channels)
            weight_parts.append(
                lax.dot_general(
                    window, flat_grad, (((0,), (0,)), ((), ())), preferred_element_type=jnp.float32
                )
            )
    weight_grad = lax.psum(
        jnp.stack(weight_parts).reshape(3, 3, channels, channels), ("lat", "lon")
    )
    return (input_grad.reshape(tile_lat, tile_lon, channels).astype(jnp.bfloat16), weight_grad)


def solution(mesh):
    placed = (
        P(("lat", "lon"), None),
        P(("lat", "lon"), None),
        P(("lat", "lon")),
        P(("lat", "lon")),
        P(("lat", "lon"), None),
        P(("lat", "lon")),
        P("lat", "lon", None),
        P(),
    )
    return jax.shard_map(
        shards, mesh=mesh, in_specs=placed, out_specs=(P("lat", "lon", None), P()), check_vma=False
    )
```

profile of v0, /device:TPU:0, one launch (start us, length us, event | category | flops | bytes accessed | tf_op | source)
XLA Modules:
  0.0 337.5 jit_solution(12751207130138029418)
XLA Ops:
  9.9 9.0 %reduce-window.6 = s32[32,8,128]{2,1,0:T(8,128)S(1)} reduce-window(s32[32,8,128]{2,1,0:T(8,128)S(1)} %fusion.91, s32[]{:T(128)} %constant.163.clone.1), window={size=1x1x128 pad=0_0x0_0x127_0}, to_apply=%region_0.1 | reduce-window | flops 4161536 | bytes 262148 | tf_op jit(solution)/shard_map/reduce-window
  21.8 3.3 scatter_custom_fusion
  26.1 7.3 %all-to-all-start = ((bf16[32,2,128]{2,1,0:T(2,128)(2,1)}), bf16[32,2,128]{2,1,0:T(2,128)(2,1)S(1)}, u32[]{:S(2)}, u32[]{:S(2)}) async-start(bf16[32,2,128]{2,1,0:T(2,128)(2,1)} %reshape.426), calls=%async_computation | async-start | bytes 32768 | tf_op jit(solution)/shard_map/all_to_all | solution.py:100
  33.4 4.3 %scatter_custom_fusion.1 = bf16[2048,128]{1,0:T(8,128)(2,1)} fusion(s32[1024]{0:T(1024)S(1)} %bitcast.220, bf16[1024,128]{1,0:T(8,128)(2,1)} %param.18, bf16[]{:T(256)} %constant.167.clone.1), kind=kCustom, calls=%fused_computation.79 | custom fusion | bytes 524800 | tf_op jit(solution)/shard_map/scatter | solution.py:76
  37.8 2.8 all-to-all-done
  40.5 3.1 all-to-all-start.1
  47.3 5.0 %collective-permute-done.4 = bf16[1,128,128]{2,1,0:T(8,128)(2,1)S(1)} collective-permute-done((bf16[1,128,128]{2,1,0:T(8,128)(2,1)S(1)}, bf16[1,128,128]{2,1,0:T(8,128)(2,1)S(1)}, u32[]{:S(2)}, u32[]{:S(2)}) %collective-permute-start.4) | collective-permute-done | bytes 32800 | tf_op jit(solution)/shard_map/ppermute | solution.py:18
  54.4 3.5 %collective-permute-start.7 = (bf16[66,1,128]{2,1,0:T(2,128)(2,1)S(1)}, bf16[66,1,128]{2,1,0:T(2,128)(2,1)S(1)}, u32[]{:S(2)}, u32[]{:S(2)}) collective-permute-start(bf16[66,1,128]{2,1,0:T(2,128)(2,1)S(1)} %get-tuple-element.167), channel_id=1, source_target_pairs={{1,0},{2,1},{3,2},{4,3},{5,4},{6,5},{7,6},{0,7},{9,8},{10,9},{11,1... | collective-permute-start | bytes 50696 | tf_op jit(solution)/shard_map/ppermute | solution.py:20
  60.2 92.0 %while.17 = (s32[]{:T(128)}, f32[72,17408]{1,0:T(8,128)}, f32[8,256,4]{1,0,2:T(8,128)S(1)}, bf16[8,256,128]{2,1,0:T(8,128)(2,1)S(1)}, s32[]{:T(128)}, /*index=5*/s32[]{:T(128)}) while((s32[]{:T(128)}, f32[72,17408]{1,0:T(8,128)}, f32[8,256,4]{1,0,2:T(8,128)S(1)}, bf16[8,256,128]{2,1,0:T(8,128)(2,1)S(1)}, s32[]{:T(128)}, ...), condition=%wide.region_8.9_spmd.clone, body=%wide.region_5.8_spmd.clone.sunk | while | flops 649949696 | bytes 63590632 | solution.py:129
  60.7 5.2 %broadcast_multiply_fusion.2 = bf16[256,136,128]{2,1,0:T(8,128)(2,1)S(1)} fusion(bf16[256,128]{1,0:T(8,128)(2,1)S(1)} %dynamic-slice_bitcast_fusion.2, bf16[256,136]{1,0:T(8,128)(2,1)S(1)} %copy.114), kind=kLoop, calls=%fused_computation.5.clone.1 | loop fusion | flops 4456448 | bytes 9048064 | tf_op jit(solution)/shard_map/while/body/eval_jaxpr/mul | solution.py:121
  65.9 3.6 %convolution_add_fusion.10 = f32[72,17408]{1,0:T(8,128)S(1)} fusion(bf16[32,8,136,128]{3,2,1,0:T(8,128)(2,1)S(1)} %bitcast.180, f32[72,17408]{1,0:T(8,128)S(1)} %bitcast.182, pred[]{:T(512)S(6)} %compare.25, bf16[256,72]{0,1:T(8,128)(2,1)S(1)} %select_reduce_fusion.5), kind=kOutput, calls=%fused_computation.2.clone.1 | convolution fusion | flops 644235264 | bytes 18976768 | tf_op jit(solution)/shard_map/while/body/eval_jaxpr/dot_general | solution.py:124
  72.2 5.2 %broadcast_multiply_fusion.2 = bf16[256,136,128]{2,1,0:T(8,128)(2,1)S(1)} fusion(bf16[256,128]{1,0:T(8,128)(2,1)S(1)} %dynamic-slice_bitcast_fusion.2, bf16[256,136]{1,0:T(8,128)(2,1)S(1)} %copy.114), kind=kLoop, calls=%fused_computation.5.clone.1 | loop fusion | flops 4456448 | bytes 9048064 | tf_op jit(solution)/shard_map/while/body/eval_jaxpr/mul | solution.py:121
  77.4 3.6 %convolution_add_fusion.10 = f32[72,17408]{1,0:T(8,128)S(1)} fusion(bf16[32,8,136,128]{3,2,1,0:T(8,128)(2,1)S(1)} %bitcast.180, f32[72,17408]{1,0:T(8,128)S(1)} %bitcast.182, pred[]{:T(512)S(6)} %compare.25, bf16[256,72]{0,1:T(8,128)(2,1)S(1)} %select_reduce_fusion.5), kind=kOutput, calls=%fused_computation.2.clone.1 | convolution fusion | flops 644235264 | bytes 18976768 | tf_op jit(solution)/shard_map/while/body/eval_jaxpr/dot_general | solution.py:124
  83.7 5.2 %broadcast_multiply_fusion.2 = bf16[256,136,128]{2,1,0:T(8,128)(2,1)S(1)} fusion(bf16[256,128]{1,0:T(8,128)(2,1)S(1)} %dynamic-slice_bitcast_fusion.2, bf16[256,136]{1,0:T(8,128)(2,1)S(1)} %copy.114), kind=kLoop, calls=%fused_computation.5.clone.1 | loop fusion | flops 4456448 | bytes 9048064 | tf_op jit(solution)/shard_map/while/body/eval_jaxpr/mul | solution.py:121
  88.9 3.6 %convolution_add_fusion.10 = f32[72,17408]{1,0:T(8,128)S(1)} fusion(bf16[32,8,136,128]{3,2,1,0:T(8,128)(2,1)S(1)} %bitcast.180, f32[72,17408]{1,0:T(8,128)S(1)} %bitcast.182, pred[]{:T(512)S(6)} %compare.25, bf16[256,72]{0,1:T(8,128)(2,1)S(1)} %select_reduce_fusion.5), kind=kOutput, calls=%fused_computation.2.clone.1 | convolution fusion | flops 644235264 | bytes 18976768 | tf_op jit(solution)/shard_map/while/body/eval_jaxpr/dot_general | solution.py:124
  95.2 5.2 %broadcast_multiply_fusion.2 = bf16[256,136,128]{2,1,0:T(8,128)(2,1)S(1)} fusion(bf16[256,128]{1,0:T(8,128)(2,1)S(1)} %dynamic-slice_bitcast_fusion.2, bf16[256,136]{1,0:T(8,128)(2,1)S(1)} %copy.114), kind=kLoop, calls=%fused_computation.5.clone.1 | loop fusion | flops 4456448 | bytes 9048064 | tf_op jit(solution)/shard_map/while/body/eval_jaxpr/mul | solution.py:121
  100.4 3.6 %convolution_add_fusion.10 = f32[72,17408]{1,0:T(8,128)S(1)} fusion(bf16[32,8,136,128]{3,2,1,0:T(8,128)(2,1)S(1)} %bitcast.180, f32[72,17408]{1,0:T(8,128)S(1)} %bitcast.182, pred[]{:T(512)S(6)} %compare.25, bf16[256,72]{0,1:T(8,128)(2,1)S(1)} %select_reduce_fusion.5), kind=kOutput, calls=%fused_computation.2.clone.1 | convolution fusion | flops 644235264 | bytes 18976768 | tf_op jit(solution)/shard_map/while/body/eval_jaxpr/dot_general | solution.py:124
  106.7 5.2 %broadcast_multiply_fusion.2 = bf16[256,136,128]{2,1,0:T(8,128)(2,1)S(1)} fusion(bf16[256,128]{1,0:T(8,128)(2,1)S(1)} %dynamic-slice_bitcast_fusion.2, bf16[256,136]{1,0:T(8,128)(2,1)S(1)} %copy.114), kind=kLoop, calls=%fused_computation.5.clone.1 | loop fusion | flops 4456448 | bytes 9048064 | tf_op jit(solution)/shard_map/while/body/eval_jaxpr/mul | solution.py:121
  111.9 3.6 %convolution_add_fusion.10 = f32[72,17408]{1,0:T(8,128)S(1)} fusion(bf16[32,8,136,128]{3,2,1,0:T(8,128)(2,1)S(1)} %bitcast.180, f32[72,17408]{1,0:T(8,128)S(1)} %bitcast.182, pred[]{:T(512)S(6)} %compare.25, bf16[256,72]{0,1:T(8,128)(2,1)S(1)} %select_reduce_fusion.5), kind=kOutput, calls=%fused_computation.2.clone.1 | convolution fusion | flops 644235264 | bytes 18976768 | tf_op jit(solution)/shard_map/while/body/eval_jaxpr/dot_general | solution.py:124
  118.2 5.2 %broadcast_multiply_fusion.2 = bf16[256,136,128]{2,1,0:T(8,128)(2,1)S(1)} fusion(bf16[256,128]{1,0:T(8,128)(2,1)S(1)} %dynamic-slice_bitcast_fusion.2, bf16[256,136]{1,0:T(8,128)(2,1)S(1)} %copy.114), kind=kLoop, calls=%fused_computation.5.clone.1 | loop fusion | flops 4456448 | bytes 9048064 | tf_op jit(solution)/shard_map/while/body/eval_jaxpr/mul | solution.py:121
  123.4 3.6 %convolution_add_fusion.10 = f32[72,17408]{1,0:T(8,128)S(1)} fusion(bf16[32,8,136,128]{3,2,1,0:T(8,128)(2,1)S(1)} %bitcast.180, f32[72,17408]{1,0:T(8,128)S(1)} %bitcast.182, pred[]{:T(512)S(6)} %compare.25, bf16[256,72]{0,1:T(8,128)(2,1)S(1)} %select_reduce_fusion.5), kind=kOutput, calls=%fused_computation.2.clone.1 | convolution fusion | flops 644235264 | bytes 18976768 | tf_op jit(solution)/shard_map/while/body/eval_jaxpr/dot_general | solution.py:124
  129.7 5.2 %broadcast_multiply_fusion.2 = bf16[256,136,128]{2,1,0:T(8,128)(2,1)S(1)} fusion(bf16[256,128]{1,0:T(8,128)(2,1)S(1)} %dynamic-slice_bitcast_fusion.2, bf16[256,136]{1,0:T(8,128)(2,1)S(1)} %copy.114), kind=kLoop, calls=%fused_computation.5.clone.1 | loop fusion | flops 4456448 | bytes 9048064 | tf_op jit(solution)/shard_map/while/body/eval_jaxpr/mul | solution.py:121
  134.9 3.6 %convolution_add_fusion.10 = f32[72,17408]{1,0:T(8,128)S(1)} fusion(bf16[32,8,136,128]{3,2,1,0:T(8,128)(2,1)S(1)} %bitcast.180, f32[72,17408]{1,0:T(8,128)S(1)} %bitcast.182, pred[]{:T(512)S(6)} %compare.25, bf16[256,72]{0,1:T(8,128)(2,1)S(1)} %select_reduce_fusion.5), kind=kOutput, calls=%fused_computation.2.clone.1 | convolution fusion | flops 644235264 | bytes 18976768 | tf_op jit(solution)/shard_map/while/body/eval_jaxpr/dot_general | solution.py:124
  141.2 5.2 %broadcast_multiply_fusion.2 = bf16[256,136,128]{2,1,0:T(8,128)(2,1)S(1)} fusion(bf16[256,128]{1,0:T(8,128)(2,1)S(1)} %dynamic-slice_bitcast_fusion.2, bf16[256,136]{1,0:T(8,128)(2,1)S(1)} %copy.114), kind=kLoop, calls=%fused_computation.5.clone.1 | loop fusion | flops 4456448 | bytes 9048064 | tf_op jit(solution)/shard_map/while/body/eval_jaxpr/mul | solution.py:121
  146.4 3.6 %convolution_add_fusion.10 = f32[72,17408]{1,0:T(8,128)S(1)} fusion(bf16[32,8,136,128]{3,2,1,0:T(8,128)(2,1)S(1)} %bitcast.180, f32[72,17408]{1,0:T(8,128)S(1)} %bitcast.182, pred[]{:T(512)S(6)} %compare.25, bf16[256,72]{0,1:T(8,128)(2,1)S(1)} %select_reduce_fusion.5), kind=kOutput, calls=%fused_computation.2.clone.1 | convolution fusion | flops 644235264 | bytes 18976768 | tf_op jit(solution)/shard_map/while/body/eval_jaxpr/dot_general | solution.py:124
  153.6 2.8 convert.24
  160.1 4.6 %collective-permute-start = (bf16[5,136,128]{2,1,0:T(8,128)(2,1)S(1)}, bf16[5,136,128]{2,1,0:T(8,128)(2,1)S(1)}, u32[]{:S(2)}, u32[]{:S(2)}) collective-permute-start(bf16[5,136,128]{2,1,0:T(8,128)(2,1)S(1)} %bitcast.193), channel_id=1, source_target_pairs={{0,8},{8,16},{16,24},{1,9},{9,17},{17,25},{2,10},{10,18},{18,26},{... | collective-permute-start | bytes 522248 | tf_op jit(solution)/shard_map/ppermute | solution.py:18
  164.7 2.7 collective-permute-done.1
  168.9 3.5 %collective-permute-start.3 = (bf16[66,5,128]{2,1,0:T(8,128)(2,1)S(1)}, bf16[66,5,128]{2,1,0:T(8,128)(2,1)S(1)}, u32[]{:S(2)}, u32[]{:S(2)}) collective-permute-start(bf16[66,5,128]{2,1,0:T(8,128)(2,1)S(1)} %get-tuple-element.165), channel_id=1, source_target_pairs={{1,0},{2,1},{3,2},{4,3},{5,4},{6,5},{7,6},{0,7},{9,8},{10,9},{11,1... | collective-permute-start | bytes 253448 | tf_op jit(solution)/shard_map/ppermute | solution.py:20
  176.4 3.1 maximum_select_fusion.1
  179.5 7.0 %fusion.126 = (bf16[64,128,128]{2,1,0:T(8,128)(2,1)}, bf16[64,128,128]{2,1,0:T(8,128)(2,1)S(1)}, bf16[64,128,128]{2,1,0:T(8,128)(2,1)}, bf16[64,128,128]{2,1,0:T...) fusion(bf16[66,130,128]{2,1,0:T(8,128)(2,1)S(1)} %get-tuple-ele, ...), kind=kLoop, calls=%fused_computation.152 | loop fusion | bytes 37748736 | tf_op jit(solution)/shard_map/slice | solution.py:160
  212.8 116.0 %all-reduce.2.cloned.1.call-done = f32[3,3,128,128]{3,2,1,0:T(8,128)} async-done(((f32[3,3,128,128]{3,2,1,0:T(8,128)}), f32[3,3,128,128]{3,2,1,0:T(8,128)}) %all-reduce.2.cloned.1.call-update) | async-done | bytes 589840 | tf_op jit(solution)/shard_map/psum | solution.py:175
  (244 shorter events, 73.5 us)
Async XLA Ops:
  26.1 14.4 %all-to-all-start = ((bf16[32,2,128]{2,1,0:T(2,128)(2,1)}), bf16[32,2,128]{2,1,0:T(2,128)(2,1)S(1)}, u32[]{:S(2)}, u32[]{:S(2)}) async-start(bf16[32,2,128]{2,1,0:T(2,128)(2,1)} %reshape.426), calls=%async_computation | async-start | bytes 32768 | tf_op jit(solution)/shard_map/all_to_all | solution.py:100
  40.5 19.7 %all-to-all-start.1 = ((bf16[32,64,128]{2,1,0:T(8,128)(2,1)}), bf16[32,64,128]{2,1,0:T(8,128)(2,1)S(1)}, u32[]{:S(2)}, u32[]{:S(2)}) async-start(bf16[32,64,128]{2,1,0:T(8,128)(2,1)} %bitcast.8), calls=%async_computation.1 | async-start | bytes 1048576 | tf_op jit(solution)/shard_map/all_to_all | solution.py:93
  43.6 285.1 %all-reduce.2.cloned.1.call-start = ((), (), s32[]{:S(2)}) async-start(), calls=%async_computation.2 | async-start | bytes 1179648 | tf_op jit(solution)/shard_map/psum | solution.py:175
  44.4 9.8 %collective-permute-start.5 = (bf16[1,128,128]{2,1,0:T(8,128)(2,1)S(1)}, bf16[1,128,128]{2,1,0:T(8,128)(2,1)S(1)}, u32[]{:S(2)}, u32[]{:S(2)}) collective-permute-start(bf16[1,128,128]{2,1,0:T(8,128)(2,1)S(1)} %get-tuple-element.168), channel_id=1, source_target_pairs={{8,0},{16,8},{24,16},{0,24},{9,1},{17,9},{25,17},{1,25},{10,2},{18... | collective-permute-start | bytes 98312 | tf_op jit(solution)/shard_map/ppermute | solution.py:20
  47.1 5.2 %collective-permute-start.4 = (bf16[1,128,128]{2,1,0:T(8,128)(2,1)S(1)}, bf16[1,128,128]{2,1,0:T(8,128)(2,1)S(1)}, u32[]{:S(2)}, u32[]{:S(2)}) collective-permute-start(bf16[1,128,128]{2,1,0:T(8,128)(2,1)S(1)} %get-tuple-element.169), channel_id=1, source_target_pairs={{0,8},{8,16},{16,24},{24,0},{1,9},{9,17},{17,25},{25,1},{2,10},{10... | collective-permute-start | bytes 98312 | tf_op jit(solution)/shard_map/ppermute | solution.py:18
  54.3 122.0 %collective-permute-start.6 = (bf16[66,1,128]{2,1,0:T(2,128)(2,1)S(1)}, bf16[66,1,128]{2,1,0:T(2,128)(2,1)S(1)}, u32[]{:S(2)}, u32[]{:S(2)}) collective-permute-start(bf16[66,1,128]{2,1,0:T(2,128)(2,1)S(1)} %get-tuple-element.166), channel_id=1, source_target_pairs={{0,1},{1,2},{2,3},{3,4},{4,5},{5,6},{6,7},{7,0},{8,9},{9,10},{10,1... | collective-permute-start | bytes 50696 | tf_op jit(solution)/shard_map/ppermute | solution.py:18
  54.4 121.9 %collective-permute-start.7 = (bf16[66,1,128]{2,1,0:T(2,128)(2,1)S(1)}, bf16[66,1,128]{2,1,0:T(2,128)(2,1)S(1)}, u32[]{:S(2)}, u32[]{:S(2)}) collective-permute-start(bf16[66,1,128]{2,1,0:T(2,128)(2,1)S(1)} %get-tuple-element.167), channel_id=1, source_target_pairs={{1,0},{2,1},{3,2},{4,3},{5,4},{6,5},{7,6},{0,7},{9,8},{10,9},{11,1... | collective-permute-start | bytes 50696 | tf_op jit(solution)/shard_map/ppermute | solution.py:20
  60.6 5.2 %slice-start = ((s8[5013504]{0:T(1024)(128)(4,1)}), s8[4194304]{0:T(1024)(128)(4,1)S(1)}, s32[]{:S(2)}) async-start(s8[5013504]{0:T(1024)(128)(4,1)} %bitcast.181), calls=%async_computation.3 | async-start | bytes 8388608 | tf_op jit(solution)/shard_map/while
  60.7 5.2 %slice-start.1 = ((s8[5013504]{0:T(1024)(128)(4,1)}), s8[819200]{0:T(1024)(128)(4,1)S(1)}, s32[]{:S(2)}) async-start(s8[5013504]{0:T(1024)(128)(4,1)} %bitcast.181), calls=%async_computation.4 | async-start | bytes 1638400 | tf_op jit(solution)/shard_map/while
  69.5 2.2 copy-start
  72.2 5.2 %slice-start = ((s8[5013504]{0:T(1024)(128)(4,1)}), s8[4194304]{0:T(1024)(128)(4,1)S(1)}, s32[]{:S(2)}) async-start(s8[5013504]{0:T(1024)(128)(4,1)} %bitcast.181), calls=%async_computation.3 | async-start | bytes 8388608 | tf_op jit(solution)/shard_map/while
  72.2 5.2 %slice-start.1 = ((s8[5013504]{0:T(1024)(128)(4,1)}), s8[819200]{0:T(1024)(128)(4,1)S(1)}, s32[]{:S(2)}) async-start(s8[5013504]{0:T(1024)(128)(4,1)} %bitcast.181), calls=%async_computation.4 | async-start | bytes 1638400 | tf_op jit(solution)/shard_map/while
  81.0 2.2 copy-start
  83.7 5.2 %slice-start = ((s8[5013504]{0:T(1024)(128)(4,1)}), s8[4194304]{0:T(1024)(128)(4,1)S(1)}, s32[]{:S(2)}) async-start(s8[5013504]{0:T(1024)(128)(4,1)} %bitcast.181), calls=%async_computation.3 | async-start | bytes 8388608 | tf_op jit(solution)/shard_map/while
  83.7 5.2 %slice-start.1 = ((s8[5013504]{0:T(1024)(128)(4,1)}), s8[819200]{0:T(1024)(128)(4,1)S(1)}, s32[]{:S(2)}) async-start(s8[5013504]{0:T(1024)(128)(4,1)} %bitcast.181), calls=%async_computation.4 | async-start | bytes 1638400 | tf_op jit(solution)/shard_map/while
  92.5 2.2 copy-start
  95.2 5.2 %slice-start = ((s8[5013504]{0:T(1024)(128)(4,1)}), s8[4194304]{0:T(1024)(128)(4,1)S(1)}, s32[]{:S(2)}) async-start(s8[5013504]{0:T(1024)(128)(4,1)} %bitcast.181), calls=%async_computation.3 | async-start | bytes 8388608 | tf_op jit(solution)/shard_map/while
  95.2 5.2 %slice-start.1 = ((s8[5013504]{0:T(1024)(128)(4,1)}), s8[819200]{0:T(1024)(128)(4,1)S(1)}, s32[]{:S(2)}) async-start(s8[5013504]{0:T(1024)(128)(4,1)} %bitcast.181), calls=%async_computation.4 | async-start | bytes 1638400 | tf_op jit(solution)/shard_map/while
  106.7 5.2 %slice-start = ((s8[5013504]{0:T(1024)(128)(4,1)}), s8[4194304]{0:T(1024)(128)(4,1)S(1)}, s32[]{:S(2)}) async-start(s8[5013504]{0:T(1024)(128)(4,1)} %bitcast.181), calls=%async_computation.3 | async-start | bytes 8388608 | tf_op jit(solution)/shard_map/while
  106.7 5.2 %slice-start.1 = ((s8[5013504]{0:T(1024)(128)(4,1)}), s8[819200]{0:T(1024)(128)(4,1)S(1)}, s32[]{:S(2)}) async-start(s8[5013504]{0:T(1024)(128)(4,1)} %bitcast.181), calls=%async_computation.4 | async-start | bytes 1638400 | tf_op jit(solution)/shard_map/while
  118.2 5.2 %slice-start = ((s8[5013504]{0:T(1024)(128)(4,1)}), s8[4194304]{0:T(1024)(128)(4,1)S(1)}, s32[]{:S(2)}) async-start(s8[5013504]{0:T(1024)(128)(4,1)} %bitcast.181), calls=%async_computation.3 | async-start | bytes 8388608 | tf_op jit(solution)/shard_map/while
  118.2 5.2 %slice-start.1 = ((s8[5013504]{0:T(1024)(128)(4,1)}), s8[819200]{0:T(1024)(128)(4,1)S(1)}, s32[]{:S(2)}) async-start(s8[5013504]{0:T(1024)(128)(4,1)} %bitcast.181), calls=%async_computation.4 | async-start | bytes 1638400 | tf_op jit(solution)/shard_map/while
  129.7 5.2 %slice-start = ((s8[5013504]{0:T(1024)(128)(4,1)}), s8[4194304]{0:T(1024)(128)(4,1)S(1)}, s32[]{:S(2)}) async-start(s8[5013504]{0:T(1024)(128)(4,1)} %bitcast.181), calls=%async_computation.3 | async-start | bytes 8388608 | tf_op jit(solution)/shard_map/while
  129.7 5.2 %slice-start.1 = ((s8[5013504]{0:T(1024)(128)(4,1)}), s8[819200]{0:T(1024)(128)(4,1)S(1)}, s32[]{:S(2)}) async-start(s8[5013504]{0:T(1024)(128)(4,1)} %bitcast.181), calls=%async_computation.4 | async-start | bytes 1638400 | tf_op jit(solution)/shard_map/while
  141.2 5.2 %slice-start = ((s8[5013504]{0:T(1024)(128)(4,1)}), s8[4194304]{0:T(1024)(128)(4,1)S(1)}, s32[]{:S(2)}) async-start(s8[5013504]{0:T(1024)(128)(4,1)} %bitcast.181), calls=%async_computation.3 | async-start | bytes 8388608 | tf_op jit(solution)/shard_map/while
  141.2 5.2 %slice-start.1 = ((s8[5013504]{0:T(1024)(128)(4,1)}), s8[819200]{0:T(1024)(128)(4,1)S(1)}, s32[]{:S(2)}) async-start(s8[5013504]{0:T(1024)(128)(4,1)} %bitcast.181), calls=%async_computation.4 | async-start | bytes 1638400 | tf_op jit(solution)/shard_map/while
  153.6 3.9 %copy-start.1 = (f32[72,17408]{1,0:T(8,128)S(1)}, f32[72,17408]{1,0:T(8,128)}, u32[]{:S(2)}) copy-start(f32[72,17408]{1,0:T(8,128)} %get-tuple-element.103) | copy-start | bytes 15040516
  158.8 8.6 %collective-permute-start.1 = (bf16[5,136,128]{2,1,0:T(8,128)(2,1)S(1)}, bf16[5,136,128]{2,1,0:T(8,128)(2,1)S(1)}, u32[]{:S(2)}, u32[]{:S(2)}) collective-permute-start(bf16[5,136,128]{2,1,0:T(8,128)(2,1)S(1)} %bitcast.197), channel_id=1, source_target_pairs={{8,0},{16,8},{24,16},{9,1},{17,9},{25,17},{10,2},{18,10},{26,18},{... | collective-permute-start | bytes 522248 | tf_op jit(solution)/shard_map/ppermute | solution.py:20
  160.1 8.2 %collective-permute-start = (bf16[5,136,128]{2,1,0:T(8,128)(2,1)S(1)}, bf16[5,136,128]{2,1,0:T(8,128)(2,1)S(1)}, u32[]{:S(2)}, u32[]{:S(2)}) collective-permute-start(bf16[5,136,128]{2,1,0:T(8,128)(2,1)S(1)} %bitcast.193), channel_id=1, source_target_pairs={{0,8},{8,16},{16,24},{1,9},{9,17},{17,25},{2,10},{10,18},{18,26},{... | collective-permute-start | bytes 522248 | tf_op jit(solution)/shard_map/ppermute | solution.py:18
  168.8 6.6 %collective-permute-start.2 = (bf16[66,5,128]{2,1,0:T(8,128)(2,1)S(1)}, bf16[66,5,128]{2,1,0:T(8,128)(2,1)S(1)}, u32[]{:S(2)}, u32[]{:S(2)}) collective-permute-start(bf16[66,5,128]{2,1,0:T(8,128)(2,1)S(1)} %get-tuple-element.164), channel_id=1, source_target_pairs={{0,1},{1,2},{2,3},{3,4},{4,5},{5,6},{6,7},{7,0},{8,9},{9,10},{10,1... | collective-permute-start | bytes 253448 | tf_op jit(solution)/shard_map/ppermute | solution.py:18
  168.9 6.5 %collective-permute-start.3 = (bf16[66,5,128]{2,1,0:T(8,128)(2,1)S(1)}, bf16[66,5,128]{2,1,0:T(8,128)(2,1)S(1)}, u32[]{:S(2)}, u32[]{:S(2)}) collective-permute-start(bf16[66,5,128]{2,1,0:T(8,128)(2,1)S(1)} %get-tuple-element.165), channel_id=1, source_target_pairs={{1,0},{2,1},{3,2},{4,3},{5,4},{6,5},{7,6},{0,7},{9,8},{10,9},{11,1... | collective-permute-start | bytes 253448 | tf_op jit(solution)/shard_map/ppermute | solution.py:20
  197.9 2.5 copy-start.7
  (13 other events, 23.9 us)
Sparse Core Ops, SparseCore 0:
  198.0 130.6 all-reduce.1
where the time goes:
time: 338 us; the launch traced here: 337 us
  waiting for transfers between devices  132 us (39%)
  other arithmetic  64.7 us (19%)
  local copies, waits for them, and re-layouts  50.3 us (15%)
  matrix products  48.7 us (14%)
  starting transfers between devices  26.1 us (8%)
  between operations  15.1 us (4%)
    psum x1, waiting for transfers between devices, shards(): lax.psum(jnp.stack(weight_parts).reshape(3, 3, channels, channels), ('lat...  116 us
    mul x8, other arithmetic, accumulate(): lon_matrix[:, :, None] * rows_blk[:, None, :]  41.4 us
    dot_general x8, matrix products, accumulate(): lax.dot_general(lat_matrix, spread, (((0,), (0,)), ((), ())), preferred_e...  28.5 us
    while x48, local copies, waits for them, and re-layouts  17.9 us
    unnamed x31, local copies, waits for them, and re-layouts  13 us
    another operation x7, other arithmetic  12.8 us
    ppermute x4, starting transfers between devices, padded_2(): lax.ppermute(head, axis, [((i + 1) % count, i) for i in range(ends)])  11 us
    dot_general x9, matrix products, shards(): lax.dot_general(window, flat_grad, (((0,), (0,)), ((), ())), preferred_el...  10.5 us
  transfers between devices with their start and end apart: 11, of which 7 were waited for; matrix products, arithmetic and copies ran while one was open for 29% of the time, Pallas kernels for 0%

commit v1 on v0

--- a/solution.py
+++ b/solution.py
@@ -3,6 +3,7 @@
 import jax.numpy as jnp
 from jax import lax
 from jax.sharding import PartitionSpec as P
+from jax.lax import psum
 
 rbf_scale = 1.5
 
@@ -172,9 +173,8 @@
                     window, flat_grad, (((0,), (0,)), ((), ())), preferred_element_type=jnp.float32
                 )
             )
-    weight_grad = lax.psum(
-        jnp.stack(weight_parts).reshape(3, 3, channels, channels), ("lat", "lon")
-    )
+    arrange_strips_all = lambda vec: psum(psum(vec, axis_name="lat"), axis_name="lon")
+    weight_grad = arrange_strips_all(jnp.stack(weight_parts).reshape(3, 3, channels, channels))
     return (input_grad.reshape(tile_lat, tile_lon, channels).astype(jnp.bfloat16), weight_grad)
 
 

time: 338 us -> 315 us (0.932)
  waiting for transfers between devices: 132 us -> 104 us
  matrix products: 48.7 us -> 53.2 us
    psum x1 -> x2, waiting for transfers between devices: 116 us -> 88.8 us  [the longest x1 54.3 us: shards(): psum(psum(vec, axis_name='lat'), axis_name='lon')]
    dot_general x9, matrix products: 9.68 us -> 14.2 us  [shards(): lax.dot_general(shifted, conv_weight[a, b], (((1,), (1,)), ((), ())), pre...]
    unnamed x31 -> x29, local copies, waits for them, and re-layouts: 13 us -> 12.3 us
  transfers between devices with their start and end apart: 11 -> 12, of which waited for: 7 -> 8; matrix products, arithmetic and copies ran while one was open for 29% -> 33% of each run, Pallas kernels for 0% -> 0%
where the time goes in v1:
time: 315 us; the launch traced here: 314 us
  waiting for transfers between devices  104 us (33%)
  other arithmetic  64.7 us (21%)
  matrix products  53.2 us (17%)
  local copies, waits for them, and re-layouts  49.6 us (16%)
  starting transfers between devices  26.4 us (8%)
  between operations  15.1 us (5%)
    psum x1, waiting for transfers between devices, shards(): psum(psum(vec, axis_name='lat'), axis_name='lon')  54.3 us
    mul x8, other arithmetic, accumulate(): lon_matrix[:, :, None] * rows_blk[:, None, :]  41.4 us
    psum x1, waiting for transfers between devices, shards(): psum(vec, axis_name='lat')  34.5 us
    dot_general x8, matrix products, accumulate(): lax.dot_general(lat_matrix, spread, (((0,), (0,)), ((), ())), preferred_e...  28.5 us
    while x48, local copies, waits for them, and re-layouts  17.8 us
    dot_general x9, matrix products, shards(): lax.dot_general(shifted, conv_weight[a, b], (((1,), (1,)), ((), ())), pre...  14.2 us
    another operation x7, other arithmetic  12.8 us
    unnamed x29, local copies, waits for them, and re-layouts  12.3 us
  transfers between devices with their start and end apart: 12, of which 8 were waited for; matrix products, arithmetic and copies ran while one was open for 33% of the time, Pallas kernels for 0%

profile of v1, /device:TPU:0, one launch (start us, length us, event | category | flops | bytes accessed | tf_op | source)
XLA Modules:
  0.0 314.5 jit_solution(12399929966287027904)
XLA Ops:
  9.9 9.0 %reduce-window.6 = s32[32,8,128]{2,1,0:T(8,128)S(1)} reduce-window(s32[32,8,128]{2,1,0:T(8,128)S(1)} %fusion.91, s32[]{:T(128)} %constant.163.clone.1), window={size=1x1x128 pad=0_0x0_0x127_0}, to_apply=%region_0.1 | reduce-window | flops 4161536 | bytes 262148 | tf_op jit(solution)/shard_map/reduce-window
  21.8 3.3 %scatter_custom_fusion = bf16[2048,4]{1,0:T(8,128)(2,1)S(1)} fusion(s32[1024]{0:T(1024)S(1)} %bitcast.219, bf16[1024,4]{1,0:T(8,128)(2,1)S(1)} %copy.67, bf16[]{:T(256)} %constant.167.clone.1), kind=kCustom, calls=%fused_computation.81 | custom fusion | bytes 16386 | tf_op jit(solution)/shard_map/scatter | solution.py:91
  26.1 7.3 %all-to-all-start = ((bf16[32,2,128]{2,1,0:T(2,128)(2,1)}), bf16[32,2,128]{2,1,0:T(2,128)(2,1)S(1)}, u32[]{:S(2)}, u32[]{:S(2)}) async-start(bf16[32,2,128]{2,1,0:T(2,128)(2,1)} %reshape.426), calls=%async_computation | async-start | bytes 32768 | tf_op jit(solution)/shard_map/all_to_all | solution.py:101
  33.4 4.3 %scatter_custom_fusion.1 = bf16[2048,128]{1,0:T(8,128)(2,1)} fusion(s32[1024]{0:T(1024)S(1)} %bitcast.220, bf16[1024,128]{1,0:T(8,128)(2,1)} %param.18, bf16[]{:T(256)} %constant.167.clone.1), kind=kCustom, calls=%fused_computation.79 | custom fusion | bytes 524800 | tf_op jit(solution)/shard_map/scatter | solution.py:77
  40.5 3.1 all-to-all-start.1
  47.3 5.0 %collective-permute-done.4 = bf16[1,128,128]{2,1,0:T(8,128)(2,1)S(1)} collective-permute-done((bf16[1,128,128]{2,1,0:T(8,128)(2,1)S(1)}, bf16[1,128,128]{2,1,0:T(8,128)(2,1)S(1)}, u32[]{:S(2)}, u32[]{:S(2)}) %collective-permute-start.4) | collective-permute-done | bytes 32800 | tf_op jit(solution)/shard_map/ppermute | solution.py:19
  54.4 3.5 %collective-permute-start.7 = (bf16[66,1,128]{2,1,0:T(2,128)(2,1)S(1)}, bf16[66,1,128]{2,1,0:T(2,128)(2,1)S(1)}, u32[]{:S(2)}, u32[]{:S(2)}) collective-permute-start(bf16[66,1,128]{2,1,0:T(2,128)(2,1)S(1)} %get-tuple-element.167), channel_id=1, source_target_pairs={{1,0},{2,1},{3,2},{4,3},{5,4},{6,5},{7,6},{0,7},{9,8},{10,9},{11,1... | collective-permute-start | bytes 50696 | tf_op jit(solution)/shard_map/ppermute | solution.py:21
  60.2 91.9 %while.17 = (s32[]{:T(128)}, f32[72,17408]{1,0:T(8,128)}, f32[8,256,4]{1,0,2:T(8,128)S(1)}, bf16[8,256,128]{2,1,0:T(8,128)(2,1)S(1)}, s32[]{:T(128)}, /*index=5*/s32[]{:T(128)}) while((s32[]{:T(128)}, f32[72,17408]{1,0:T(8,128)}, f32[8,256,4]{1,0,2:T(8,128)S(1)}, bf16[8,256,128]{2,1,0:T(8,128)(2,1)S(1)}, s32[]{:T(128)}, ...), condition=%wide.region_8.9_spmd.clone, body=%wide.region_5.8_spmd.clone.sunk | while | flops 649949696 | bytes 63590632 | solution.py:130
  60.7 5.2 %broadcast_multiply_fusion.2 = bf16[256,136,128]{2,1,0:T(8,128)(2,1)S(1)} fusion(bf16[256,128]{1,0:T(8,128)(2,1)S(1)} %dynamic-slice_bitcast_fusion.2, bf16[256,136]{1,0:T(8,128)(2,1)S(1)} %copy.114), kind=kLoop, calls=%fused_computation.5.clone.1 | loop fusion | flops 4456448 | bytes 9048064 | tf_op jit(solution)/shard_map/while/body/eval_jaxpr/mul | solution.py:122
  65.9 3.6 %convolution_add_fusion.10 = f32[72,17408]{1,0:T(8,128)S(1)} fusion(bf16[32,8,136,128]{3,2,1,0:T(8,128)(2,1)S(1)} %bitcast.180, f32[72,17408]{1,0:T(8,128)S(1)} %bitcast.182, pred[]{:T(512)S(6)} %compare.25, bf16[256,72]{0,1:T(8,128)(2,1)S(1)} %select_reduce_fusion.5), kind=kOutput, calls=%fused_computation.2.clone.1 | convolution fusion | flops 644235264 | bytes 18976768 | tf_op jit(solution)/shard_map/while/body/eval_jaxpr/dot_general | solution.py:125
  72.2 5.2 %broadcast_multiply_fusion.2 = bf16[256,136,128]{2,1,0:T(8,128)(2,1)S(1)} fusion(bf16[256,128]{1,0:T(8,128)(2,1)S(1)} %dynamic-slice_bitcast_fusion.2, bf16[256,136]{1,0:T(8,128)(2,1)S(1)} %copy.114), kind=kLoop, calls=%fused_computation.5.clone.1 | loop fusion | flops 4456448 | bytes 9048064 | tf_op jit(solution)/shard_map/while/body/eval_jaxpr/mul | solution.py:122
  77.4 3.6 %convolution_add_fusion.10 = f32[72,17408]{1,0:T(8,128)S(1)} fusion(bf16[32,8,136,128]{3,2,1,0:T(8,128)(2,1)S(1)} %bitcast.180, f32[72,17408]{1,0:T(8,128)S(1)} %bitcast.182, pred[]{:T(512)S(6)} %compare.25, bf16[256,72]{0,1:T(8,128)(2,1)S(1)} %select_reduce_fusion.5), kind=kOutput, calls=%fused_computation.2.clone.1 | convolution fusion | flops 644235264 | bytes 18976768 | tf_op jit(solution)/shard_map/while/body/eval_jaxpr/dot_general | solution.py:125
  83.7 5.2 %broadcast_multiply_fusion.2 = bf16[256,136,128]{2,1,0:T(8,128)(2,1)S(1)} fusion(bf16[256,128]{1,0:T(8,128)(2,1)S(1)} %dynamic-slice_bitcast_fusion.2, bf16[256,136]{1,0:T(8,128)(2,1)S(1)} %copy.114), kind=kLoop, calls=%fused_computation.5.clone.1 | loop fusion | flops 4456448 | bytes 9048064 | tf_op jit(solution)/shard_map/while/body/eval_jaxpr/mul | solution.py:122
  88.9 3.6 %convolution_add_fusion.10 = f32[72,17408]{1,0:T(8,128)S(1)} fusion(bf16[32,8,136,128]{3,2,1,0:T(8,128)(2,1)S(1)} %bitcast.180, f32[72,17408]{1,0:T(8,128)S(1)} %bitcast.182, pred[]{:T(512)S(6)} %compare.25, bf16[256,72]{0,1:T(8,128)(2,1)S(1)} %select_reduce_fusion.5), kind=kOutput, calls=%fused_computation.2.clone.1 | convolution fusion | flops 644235264 | bytes 18976768 | tf_op jit(solution)/shard_map/while/body/eval_jaxpr/dot_general | solution.py:125
  95.2 5.2 %broadcast_multiply_fusion.2 = bf16[256,136,128]{2,1,0:T(8,128)(2,1)S(1)} fusion(bf16[256,128]{1,0:T(8,128)(2,1)S(1)} %dynamic-slice_bitcast_fusion.2, bf16[256,136]{1,0:T(8,128)(2,1)S(1)} %copy.114), kind=kLoop, calls=%fused_computation.5.clone.1 | loop fusion | flops 4456448 | bytes 9048064 | tf_op jit(solution)/shard_map/while/body/eval_jaxpr/mul | solution.py:122
  100.4 3.6 %convolution_add_fusion.10 = f32[72,17408]{1,0:T(8,128)S(1)} fusion(bf16[32,8,136,128]{3,2,1,0:T(8,128)(2,1)S(1)} %bitcast.180, f32[72,17408]{1,0:T(8,128)S(1)} %bitcast.182, pred[]{:T(512)S(6)} %compare.25, bf16[256,72]{0,1:T(8,128)(2,1)S(1)} %select_reduce_fusion.5), kind=kOutput, calls=%fused_computation.2.clone.1 | convolution fusion | flops 644235264 | bytes 18976768 | tf_op jit(solution)/shard_map/while/body/eval_jaxpr/dot_general | solution.py:125
  106.7 5.2 %broadcast_multiply_fusion.2 = bf16[256,136,128]{2,1,0:T(8,128)(2,1)S(1)} fusion(bf16[256,128]{1,0:T(8,128)(2,1)S(1)} %dynamic-slice_bitcast_fusion.2, bf16[256,136]{1,0:T(8,128)(2,1)S(1)} %copy.114), kind=kLoop, calls=%fused_computation.5.clone.1 | loop fusion | flops 4456448 | bytes 9048064 | tf_op jit(solution)/shard_map/while/body/eval_jaxpr/mul | solution.py:122
  111.9 3.6 %convolution_add_fusion.10 = f32[72,17408]{1,0:T(8,128)S(1)} fusion(bf16[32,8,136,128]{3,2,1,0:T(8,128)(2,1)S(1)} %bitcast.180, f32[72,17408]{1,0:T(8,128)S(1)} %bitcast.182, pred[]{:T(512)S(6)} %compare.25, bf16[256,72]{0,1:T(8,128)(2,1)S(1)} %select_reduce_fusion.5), kind=kOutput, calls=%fused_computation.2.clone.1 | convolution fusion | flops 644235264 | bytes 18976768 | tf_op jit(solution)/shard_map/while/body/eval_jaxpr/dot_general | solution.py:125
  118.2 5.2 %broadcast_multiply_fusion.2 = bf16[256,136,128]{2,1,0:T(8,128)(2,1)S(1)} fusion(bf16[256,128]{1,0:T(8,128)(2,1)S(1)} %dynamic-slice_bitcast_fusion.2, bf16[256,136]{1,0:T(8,128)(2,1)S(1)} %copy.114), kind=kLoop, calls=%fused_computation.5.clone.1 | loop fusion | flops 4456448 | bytes 9048064 | tf_op jit(solution)/shard_map/while/body/eval_jaxpr/mul | solution.py:122
  123.4 3.6 %convolution_add_fusion.10 = f32[72,17408]{1,0:T(8,128)S(1)} fusion(bf16[32,8,136,128]{3,2,1,0:T(8,128)(2,1)S(1)} %bitcast.180, f32[72,17408]{1,0:T(8,128)S(1)} %bitcast.182, pred[]{:T(512)S(6)} %compare.25, bf16[256,72]{0,1:T(8,128)(2,1)S(1)} %select_reduce_fusion.5), kind=kOutput, calls=%fused_computation.2.clone.1 | convolution fusion | flops 644235264 | bytes 18976768 | tf_op jit(solution)/shard_map/while/body/eval_jaxpr/dot_general | solution.py:125
  129.6 5.2 %broadcast_multiply_fusion.2 = bf16[256,136,128]{2,1,0:T(8,128)(2,1)S(1)} fusion(bf16[256,128]{1,0:T(8,128)(2,1)S(1)} %dynamic-slice_bitcast_fusion.2, bf16[256,136]{1,0:T(8,128)(2,1)S(1)} %copy.114), kind=kLoop, calls=%fused_computation.5.clone.1 | loop fusion | flops 4456448 | bytes 9048064 | tf_op jit(solution)/shard_map/while/body/eval_jaxpr/mul | solution.py:122
  134.9 3.6 %convolution_add_fusion.10 = f32[72,17408]{1,0:T(8,128)S(1)} fusion(bf16[32,8,136,128]{3,2,1,0:T(8,128)(2,1)S(1)} %bitcast.180, f32[72,17408]{1,0:T(8,128)S(1)} %bitcast.182, pred[]{:T(512)S(6)} %compare.25, bf16[256,72]{0,1:T(8,128)(2,1)S(1)} %select_reduce_fusion.5), kind=kOutput, calls=%fused_computation.2.clone.1 | convolution fusion | flops 644235264 | bytes 18976768 | tf_op jit(solution)/shard_map/while/body/eval_jaxpr/dot_general | solution.py:125
  141.1 5.2 %broadcast_multiply_fusion.2 = bf16[256,136,128]{2,1,0:T(8,128)(2,1)S(1)} fusion(bf16[256,128]{1,0:T(8,128)(2,1)S(1)} %dynamic-slice_bitcast_fusion.2, bf16[256,136]{1,0:T(8,128)(2,1)S(1)} %copy.114), kind=kLoop, calls=%fused_computation.5.clone.1 | loop fusion | flops 4456448 | bytes 9048064 | tf_op jit(solution)/shard_map/while/body/eval_jaxpr/mul | solution.py:122
  146.3 3.6 %convolution_add_fusion.10 = f32[72,17408]{1,0:T(8,128)S(1)} fusion(bf16[32,8,136,128]{3,2,1,0:T(8,128)(2,1)S(1)} %bitcast.180, f32[72,17408]{1,0:T(8,128)S(1)} %bitcast.182, pred[]{:T(512)S(6)} %compare.25, bf16[256,72]{0,1:T(8,128)(2,1)S(1)} %select_reduce_fusion.5), kind=kOutput, calls=%fused_computation.2.clone.1 | convolution fusion | flops 644235264 | bytes 18976768 | tf_op jit(solution)/shard_map/while/body/eval_jaxpr/dot_general | solution.py:125
  153.5 2.8 convert.24
  160.0 4.6 %collective-permute-start = (bf16[5,136,128]{2,1,0:T(8,128)(2,1)S(1)}, bf16[5,136,128]{2,1,0:T(8,128)(2,1)S(1)}, u32[]{:S(2)}, u32[]{:S(2)}) collective-permute-start(bf16[5,136,128]{2,1,0:T(8,128)(2,1)S(1)} %bitcast.193), channel_id=1, source_target_pairs={{0,8},{8,16},{16,24},{1,9},{9,17},{17,25},{2,10},{10,18},{18,26},{... | collective-permute-start | bytes 522248 | tf_op jit(solution)/shard_map/ppermute | solution.py:19
  168.8 3.5 %collective-permute-start.3 = (bf16[66,5,128]{2,1,0:T(8,128)(2,1)S(1)}, bf16[66,5,128]{2,1,0:T(8,128)(2,1)S(1)}, u32[]{:S(2)}, u32[]{:S(2)}) collective-permute-start(bf16[66,5,128]{2,1,0:T(8,128)(2,1)S(1)} %get-tuple-element.165), channel_id=1, source_target_pairs={{1,0},{2,1},{3,2},{4,3},{5,4},{6,5},{7,6},{0,7},{9,8},{10,9},{11,1... | collective-permute-start | bytes 253448 | tf_op jit(solution)/shard_map/ppermute | solution.py:21
  176.3 3.1 maximum_select_fusion.1
  179.4 7.1 %fusion.126 = (bf16[64,128,128]{2,1,0:T(8,128)(2,1)}, bf16[64,128,128]{2,1,0:T(8,128)(2,1)S(1)}, bf16[64,128,128]{2,1,0:T(8,128)(2,1)}, bf16[64,128,128]{2,1,0:T...) fusion(bf16[66,130,128]{2,1,0:T(8,128)(2,1)S(1)} %get-tuple-ele, ...), kind=kLoop, calls=%fused_computation.152 | loop fusion | bytes 37748736 | tf_op jit(solution)/shard_map/slice | solution.py:161
  212.0 34.5 %all-reduce.3.cloned.1.call-done = f32[3,3,128,128]{3,2,1,0:T(8,128)} async-done(((f32[3,3,128,128]{3,2,1,0:T(8,128)}), f32[3,3,128,128]{3,2,1,0:T(8,128)}) %all-reduce.3.cloned.1.call-update) | async-done | bytes 589840 | tf_op jit(solution)/shard_map/psum | solution.py:176
  246.5 4.8 %fusion.5 = bf16[8192,128]{1,0:T(8,128)(2,1)} fusion(f32[8192,128]{1,0:T(8,128)} %convolution_add_fusion.2, bf16[8192,128]{1,0:T(8,128)(2,1)} %bitcast.192, bf16[3,3,128,128]{3,2,1,0:T(8,128)(2,1)S(1)} %copy-done.9), kind=kOutput, calls=%fused_computation.31 | convolution fusion | flops 270532608 | bytes 8421376 | tf_op jit(solution)/shard_map/dot_general | solution.py:164
  251.4 54.3 %all-reduce.5.cloned.1.call-done = f32[3,3,128,128]{3,2,1,0:T(8,128)} async-done(((f32[3,3,128,128]{3,2,1,0:T(8,128)}), f32[3,3,128,128]{3,2,1,0:T(8,128)}) %all-reduce.5.cloned.1.call-update) | async-done | bytes 589840 | tf_op jit(solution)/shard_map/psum | solution.py:176
  (245 shorter events, 78.1 us)
Async XLA Ops:
  26.1 14.4 %all-to-all-start = ((bf16[32,2,128]{2,1,0:T(2,128)(2,1)}), bf16[32,2,128]{2,1,0:T(2,128)(2,1)S(1)}, u32[]{:S(2)}, u32[]{:S(2)}) async-start(bf16[32,2,128]{2,1,0:T(2,128)(2,1)} %reshape.426), calls=%async_computation | async-start | bytes 32768 | tf_op jit(solution)/shard_map/all_to_all | solution.py:101
  40.5 19.7 %all-to-all-start.1 = ((bf16[32,64,128]{2,1,0:T(8,128)(2,1)}), bf16[32,64,128]{2,1,0:T(8,128)(2,1)S(1)}, u32[]{:S(2)}, u32[]{:S(2)}) async-start(bf16[32,64,128]{2,1,0:T(8,128)(2,1)} %bitcast.8), calls=%async_computation.1 | async-start | bytes 1048576 | tf_op jit(solution)/shard_map/all_to_all | solution.py:94
  43.6 202.9 %all-reduce.3.cloned.1.call-start = ((), (), s32[]{:S(2)}) async-start(), calls=%async_computation.2 | async-start | bytes 1179648 | tf_op jit(solution)/shard_map/psum | solution.py:176
  44.4 9.8 %collective-permute-start.5 = (bf16[1,128,128]{2,1,0:T(8,128)(2,1)S(1)}, bf16[1,128,128]{2,1,0:T(8,128)(2,1)S(1)}, u32[]{:S(2)}, u32[]{:S(2)}) collective-permute-start(bf16[1,128,128]{2,1,0:T(8,128)(2,1)S(1)} %get-tuple-element.168), channel_id=1, source_target_pairs={{8,0},{16,8},{24,16},{0,24},{9,1},{17,9},{25,17},{1,25},{10,2},{18... | collective-permute-start | bytes 98312 | tf_op jit(solution)/shard_map/ppermute | solution.py:21
  47.1 5.2 %collective-permute-start.4 = (bf16[1,128,128]{2,1,0:T(8,128)(2,1)S(1)}, bf16[1,128,128]{2,1,0:T(8,128)(2,1)S(1)}, u32[]{:S(2)}, u32[]{:S(2)}) collective-permute-start(bf16[1,128,128]{2,1,0:T(8,128)(2,1)S(1)} %get-tuple-element.169), channel_id=1, source_target_pairs={{0,8},{8,16},{16,24},{24,0},{1,9},{9,17},{17,25},{25,1},{2,10},{10... | collective-permute-start | bytes 98312 | tf_op jit(solution)/shard_map/ppermute | solution.py:19
  54.3 121.9 %collective-permute-start.6 = (bf16[66,1,128]{2,1,0:T(2,128)(2,1)S(1)}, bf16[66,1,128]{2,1,0:T(2,128)(2,1)S(1)}, u32[]{:S(2)}, u32[]{:S(2)}) collective-permute-start(bf16[66,1,128]{2,1,0:T(2,128)(2,1)S(1)} %get-tuple-element.166), channel_id=1, source_target_pairs={{0,1},{1,2},{2,3},{3,4},{4,5},{5,6},{6,7},{7,0},{8,9},{9,10},{10,1... | collective-permute-start | bytes 50696 | tf_op jit(solution)/shard_map/ppermute | solution.py:19
  54.4 121.8 %collective-permute-start.7 = (bf16[66,1,128]{2,1,0:T(2,128)(2,1)S(1)}, bf16[66,1,128]{2,1,0:T(2,128)(2,1)S(1)}, u32[]{:S(2)}, u32[]{:S(2)}) collective-permute-start(bf16[66,1,128]{2,1,0:T(2,128)(2,1)S(1)} %get-tuple-element.167), channel_id=1, source_target_pairs={{1,0},{2,1},{3,2},{4,3},{5,4},{6,5},{7,6},{0,7},{9,8},{10,9},{11,1... | collective-permute-start | bytes 50696 | tf_op jit(solution)/shard_map/ppermute | solution.py:21
  60.6 5.2 %slice-start = ((s8[5013504]{0:T(1024)(128)(4,1)}), s8[4194304]{0:T(1024)(128)(4,1)S(1)}, s32[]{:S(2)}) async-start(s8[5013504]{0:T(1024)(128)(4,1)} %bitcast.181), calls=%async_computation.4 | async-start | bytes 8388608 | tf_op jit(solution)/shard_map/while
  60.7 5.2 %slice-start.1 = ((s8[5013504]{0:T(1024)(128)(4,1)}), s8[819200]{0:T(1024)(128)(4,1)S(1)}, s32[]{:S(2)}) async-start(s8[5013504]{0:T(1024)(128)(4,1)} %bitcast.181), calls=%async_computation.5 | async-start | bytes 1638400 | tf_op jit(solution)/shard_map/while
  72.1 5.2 %slice-start = ((s8[5013504]{0:T(1024)(128)(4,1)}), s8[4194304]{0:T(1024)(128)(4,1)S(1)}, s32[]{:S(2)}) async-start(s8[5013504]{0:T(1024)(128)(4,1)} %bitcast.181), calls=%async_computation.4 | async-start | bytes 8388608 | tf_op jit(solution)/shard_map/while
  72.2 5.2 %slice-start.1 = ((s8[5013504]{0:T(1024)(128)(4,1)}), s8[819200]{0:T(1024)(128)(4,1)S(1)}, s32[]{:S(2)}) async-start(s8[5013504]{0:T(1024)(128)(4,1)} %bitcast.181), calls=%async_computation.5 | async-start | bytes 1638400 | tf_op jit(solution)/shard_map/while
  83.6 5.2 %slice-start = ((s8[5013504]{0:T(1024)(128)(4,1)}), s8[4194304]{0:T(1024)(128)(4,1)S(1)}, s32[]{:S(2)}) async-start(s8[5013504]{0:T(1024)(128)(4,1)} %bitcast.181), calls=%async_computation.4 | async-start | bytes 8388608 | tf_op jit(solution)/shard_map/while
  83.7 5.2 %slice-start.1 = ((s8[5013504]{0:T(1024)(128)(4,1)}), s8[819200]{0:T(1024)(128)(4,1)S(1)}, s32[]{:S(2)}) async-start(s8[5013504]{0:T(1024)(128)(4,1)} %bitcast.181), calls=%async_computation.5 | async-start | bytes 1638400 | tf_op jit(solution)/shard_map/while
  95.1 5.2 %slice-start = ((s8[5013504]{0:T(1024)(128)(4,1)}), s8[4194304]{0:T(1024)(128)(4,1)S(1)}, s32[]{:S(2)}) async-start(s8[5013504]{0:T(1024)(128)(4,1)} %bitcast.181), calls=%async_computation.4 | async-start | bytes 8388608 | tf_op jit(solution)/shard_map/while
  95.2 5.2 %slice-start.1 = ((s8[5013504]{0:T(1024)(128)(4,1)}), s8[819200]{0:T(1024)(128)(4,1)S(1)}, s32[]{:S(2)}) async-start(s8[5013504]{0:T(1024)(128)(4,1)} %bitcast.181), calls=%async_computation.5 | async-start | bytes 1638400 | tf_op jit(solution)/shard_map/while
  103.9 2.2 copy-start
  106.6 5.2 %slice-start = ((s8[5013504]{0:T(1024)(128)(4,1)}), s8[4194304]{0:T(1024)(128)(4,1)S(1)}, s32[]{:S(2)}) async-start(s8[5013504]{0:T(1024)(128)(4,1)} %bitcast.181), calls=%async_computation.4 | async-start | bytes 8388608 | tf_op jit(solution)/shard_map/while
  106.7 5.2 %slice-start.1 = ((s8[5013504]{0:T(1024)(128)(4,1)}), s8[819200]{0:T(1024)(128)(4,1)S(1)}, s32[]{:S(2)}) async-start(s8[5013504]{0:T(1024)(128)(4,1)} %bitcast.181), calls=%async_computation.5 | async-start | bytes 1638400 | tf_op jit(solution)/shard_map/while
  118.1 5.2 %slice-start = ((s8[5013504]{0:T(1024)(128)(4,1)}), s8[4194304]{0:T(1024)(128)(4,1)S(1)}, s32[]{:S(2)}) async-start(s8[5013504]{0:T(1024)(128)(4,1)} %bitcast.181), calls=%async_computation.4 | async-start | bytes 8388608 | tf_op jit(solution)/shard_map/while
  118.1 5.2 %slice-start.1 = ((s8[5013504]{0:T(1024)(128)(4,1)}), s8[819200]{0:T(1024)(128)(4,1)S(1)}, s32[]{:S(2)}) async-start(s8[5013504]{0:T(1024)(128)(4,1)} %bitcast.181), calls=%async_computation.5 | async-start | bytes 1638400 | tf_op jit(solution)/shard_map/while
  129.6 5.2 %slice-start = ((s8[5013504]{0:T(1024)(128)(4,1)}), s8[4194304]{0:T(1024)(128)(4,1)S(1)}, s32[]{:S(2)}) async-start(s8[5013504]{0:T(1024)(128)(4,1)} %bitcast.181), calls=%async_computation.4 | async-start | bytes 8388608 | tf_op jit(solution)/shard_map/while
  129.6 5.2 %slice-start.1 = ((s8[5013504]{0:T(1024)(128)(4,1)}), s8[819200]{0:T(1024)(128)(4,1)S(1)}, s32[]{:S(2)}) async-start(s8[5013504]{0:T(1024)(128)(4,1)} %bitcast.181), calls=%async_computation.5 | async-start | bytes 1638400 | tf_op jit(solution)/shard_map/while
  141.1 5.2 %slice-start = ((s8[5013504]{0:T(1024)(128)(4,1)}), s8[4194304]{0:T(1024)(128)(4,1)S(1)}, s32[]{:S(2)}) async-start(s8[5013504]{0:T(1024)(128)(4,1)} %bitcast.181), calls=%async_computation.4 | async-start | bytes 8388608 | tf_op jit(solution)/shard_map/while
  141.1 5.2 %slice-start.1 = ((s8[5013504]{0:T(1024)(128)(4,1)}), s8[819200]{0:T(1024)(128)(4,1)S(1)}, s32[]{:S(2)}) async-start(s8[5013504]{0:T(1024)(128)(4,1)} %bitcast.181), calls=%async_computation.5 | async-start | bytes 1638400 | tf_op jit(solution)/shard_map/while
  153.5 3.9 %copy-start.1 = (f32[72,17408]{1,0:T(8,128)S(1)}, f32[72,17408]{1,0:T(8,128)}, u32[]{:S(2)}) copy-start(f32[72,17408]{1,0:T(8,128)} %get-tuple-element.103) | copy-start | bytes 15040516
  158.7 8.6 %collective-permute-start.1 = (bf16[5,136,128]{2,1,0:T(8,128)(2,1)S(1)}, bf16[5,136,128]{2,1,0:T(8,128)(2,1)S(1)}, u32[]{:S(2)}, u32[]{:S(2)}) collective-permute-start(bf16[5,136,128]{2,1,0:T(8,128)(2,1)S(1)} %bitcast.197), channel_id=1, source_target_pairs={{8,0},{16,8},{24,16},{9,1},{17,9},{25,17},{10,2},{18,10},{26,18},{... | collective-permute-start | bytes 522248 | tf_op jit(solution)/shard_map/ppermute | solution.py:21
  160.0 8.2 %collective-permute-start = (bf16[5,136,128]{2,1,0:T(8,128)(2,1)S(1)}, bf16[5,136,128]{2,1,0:T(8,128)(2,1)S(1)}, u32[]{:S(2)}, u32[]{:S(2)}) collective-permute-start(bf16[5,136,128]{2,1,0:T(8,128)(2,1)S(1)} %bitcast.193), channel_id=1, source_target_pairs={{0,8},{8,16},{16,24},{1,9},{9,17},{17,25},{2,10},{10,18},{18,26},{... | collective-permute-start | bytes 522248 | tf_op jit(solution)/shard_map/ppermute | solution.py:19
  168.7 6.6 %collective-permute-start.2 = (bf16[66,5,128]{2,1,0:T(8,128)(2,1)S(1)}, bf16[66,5,128]{2,1,0:T(8,128)(2,1)S(1)}, u32[]{:S(2)}, u32[]{:S(2)}) collective-permute-start(bf16[66,5,128]{2,1,0:T(8,128)(2,1)S(1)} %get-tuple-element.164), channel_id=1, source_target_pairs={{0,1},{1,2},{2,3},{3,4},{4,5},{5,6},{6,7},{7,0},{8,9},{9,10},{10,1... | collective-permute-start | bytes 253448 | tf_op jit(solution)/shard_map/ppermute | solution.py:19
  168.8 6.5 %collective-permute-start.3 = (bf16[66,5,128]{2,1,0:T(8,128)(2,1)S(1)}, bf16[66,5,128]{2,1,0:T(8,128)(2,1)S(1)}, u32[]{:S(2)}, u32[]{:S(2)}) collective-permute-start(bf16[66,5,128]{2,1,0:T(8,128)(2,1)S(1)} %get-tuple-element.165), channel_id=1, source_target_pairs={{1,0},{2,1},{3,2},{4,3},{5,4},{6,5},{7,6},{0,7},{9,8},{10,9},{11,1... | collective-permute-start | bytes 253448 | tf_op jit(solution)/shard_map/ppermute | solution.py:21
  195.6 2.5 copy-start.9
  197.8 107.9 %all-reduce.5.cloned.1.call-start = ((), (), s32[]{:S(2)}) async-start(), calls=%async_computation.3 | async-start | bytes 1179648 | tf_op jit(solution)/shard_map/psum | solution.py:176
  198.1 2.5 copy-start.7
  (13 other events, 24.4 us)
Sparse Core Ops, SparseCore 0:
  198.0 48.5 all-reduce.2
  248.9 56.7 all-reduce.4
